TPU v7x, 128 devices: a whole 4x4x4 slice. The times are simulated.
128 devices in a mesh: ctx: 16 (over y_hi, x, core), tp: 8 (over y_lo, z).
Axes of the slice: x: 4, y: 4 (y_hi: 2, y_lo: 2; y = y_hi * 2 + y_lo), z: 4, core: 2. Of those that a mesh axis runs over, the one named last changes fastest.
Arguments:
- tokens: bfloat16 [2048, 4096], P('ctx', 'tp'), may hold values from -6 to 6
- in_weight: bfloat16 [4096, 3, 4096], P(None, None, 'tp'), may hold values from -0.09375 to 0.09375
- conv_weight: float32 [7, 3, 4096], P(None, None, 'tp'), may hold values from -2 to 2
- filters: bfloat16 [2048, 4096], P(None, 'tp'), may hold values from -1 to 1
- skip_gain: float32 [4096], P('tp'), may hold values from -4 to 4
Outputs:
- mixed_out: bfloat16 [2048, 4096], P('ctx', 'tp')
All inputs are finite; a program needn't handle non-finite values.
Results may differ from a plain program's by a relative error of at most 0.0095.
Values may be sent and summed in bfloat16 or wider, within the bound.
A program may use at most 128 MiB of HBM per device.

v0:
```python
import math

import jax
import jax.numpy as jnp
from jax import lax
from jax.sharding import PartitionSpec as P

TAPS = 7


def passed_along(value, axis, steps):
    count = lax.axis_size(axis)
    leading, last = (max(0, -steps), min(count, count - steps))
    return lax.ppermute(value, axis, [(source, source + steps) for source in range(leading, last)])


def exact_dot(left, right):
    return jnp.dot(left, right, precision=lax.Precision.HIGHEST, preferred_element_type=jnp.float32)


def split_table(table):
    high = table.astype(jnp.bfloat16)
    low = (table - high.astype(jnp.float32)).astype(jnp.bfloat16)
    return (high, low)


def local(tokens, in_weight, conv_weight, filters, skip_gain):
    block_rows = tokens.shape[0]
    channels = in_weight.shape[2]
    flat_weight = in_weight.reshape(in_weight.shape[0], 3 * channels)
    gathered = lax.all_gather(tokens, "tp", axis=1, tiled=True)
    summed = jnp.dot(gathered, flat_weight, preferred_element_type=jnp.float32)
    projected = summed.astype(jnp.bfloat16).reshape(block_rows, 3, channels)
    earlier = passed_along(projected[block_rows - (TAPS - 1) :], "ctx", 1)
    extended = jnp.concatenate([earlier, projected], 0).astype(jnp.float32)
    branches = conv_weight[0] * extended[0:block_rows]
    for tap_index in range(1, TAPS):
        branches = branches + conv_weight[tap_index] * extended[tap_index : tap_index + block_rows]
    gate_branch = branches[:, 0]
    product = (branches[:, 1] * branches[:, 2]).astype(jnp.bfloat16)
    product_wide = product.astype(jnp.float32)
    sub_rows = block_rows // 2
    dft_length = 2 * sub_rows
    frequency = jnp.arange(sub_rows, dtype=jnp.int32)
    position = jnp.arange(sub_rows, dtype=jnp.int32)
    step_angle = 2.0 * math.pi / dft_length
    angles = (frequency[:, None] * position[None, :] % dft_length).astype(jnp.float32) * step_angle
    cos_high, cos_low = split_table(jnp.cos(angles))
    sin_high, sin_low = split_table(-jnp.sin(angles))
    alternate = jnp.where(frequency % 2 == 0, 1.0, -1.0).astype(jnp.float32)[:, None]
    nyquist_sign = jnp.where(position % 2 == 0, 1.0, -1.0).astype(jnp.bfloat16)
    nyquist_alternate = 1.0
    back_angles = ((position[:, None] + sub_rows) * frequency[None, :] % dft_length).astype(
        jnp.float32
    ) * step_angle
    back_weights = jnp.where(frequency == 0, 1.0, 2.0).astype(jnp.float32)[None, :]
    cos_back = jnp.cos(back_angles) * back_weights
    sin_back = jnp.sin(back_angles) * back_weights
    nyquist_back = jnp.where((position + sub_rows) % 2 == 0, 1.0, -1.0).astype(jnp.float32)

    def spectrum(data):
        real_part = jnp.einsum(
            "ks,hsc->hkc", cos_high, data, preferred_element_type=jnp.float32
        ) + jnp.einsum("ks,hsc->hkc", cos_low, data, preferred_element_type=jnp.float32)
        imag_part = jnp.einsum(
            "ks,hsc->hkc", sin_high, data, preferred_element_type=jnp.float32
        ) + jnp.einsum("ks,hsc->hkc", sin_low, data, preferred_element_type=jnp.float32)
        nyquist = jnp.einsum("s,hsc->hc", nyquist_sign, data, preferred_element_type=jnp.float32)
        return (real_part, imag_part, nyquist)

    blocks = filters.shape[0] // sub_rows
    filter_real, filter_imag, filter_nyquist = spectrum(filters.reshape(blocks, sub_rows, channels))
    padded_real = jnp.concatenate([jnp.zeros((1, sub_rows, channels), jnp.float32), filter_real], 0)
    padded_imag = jnp.concatenate([jnp.zeros((1, sub_rows, channels), jnp.float32), filter_imag], 0)
    padded_nyquist = jnp.concatenate([jnp.zeros((1, channels), jnp.float32), filter_nyquist], 0)
    own_index = lax.axis_index("ctx")

    def gain_at(distance):
        causal = (distance >= 0).astype(jnp.float32)
        lag_index = jnp.clip(distance, 0, blocks - 1)
        gain_real = lax.dynamic_index_in_dim(
            padded_real, lag_index, 0, keepdims=False
        ) + alternate * lax.dynamic_index_in_dim(padded_real, lag_index + 1, 0, keepdims=False)
        gain_imag = lax.dynamic_index_in_dim(
            padded_imag, lag_index, 0, keepdims=False
        ) + alternate * lax.dynamic_index_in_dim(padded_imag, lag_index + 1, 0, keepdims=False)
        gain_nyquist = lax.dynamic_index_in_dim(
            padded_nyquist, lag_index, 0, keepdims=False
        ) + nyquist_alternate * lax.dynamic_index_in_dim(
            padded_nyquist, lag_index + 1, 0, keepdims=False
        )
        return (causal * gain_real, causal * gain_imag, causal * gain_nyquist)

    def add_term(running, source_real, source_imag, source_nyquist, source_block):
        next_real, next_imag, next_nyquist = ([], [], [])
        for target in range(2):
            total_real = running[0][target]
            total_imag = running[1][target]
            total_nyquist = running[2][target]
            for half in range(2):
                gain_real, gain_imag, gain_nyquist = gain_at(
                    2 * (own_index - source_block) + target - half
                )
                total_real = (
                    total_real + gain_real * source_real[half] - gain_imag * source_imag[half]
                )
                total_imag = (
                    total_imag + gain_real * source_imag[half] + gain_imag * source_real[half]
                )
                total_nyquist = total_nyquist + gain_nyquist * source_nyquist[half]
            next_real.append(total_real)
            next_imag.append(total_imag)
            next_nyquist.append(total_nyquist)
        return (jnp.stack(next_real), jnp.stack(next_imag), jnp.stack(next_nyquist))

    initial = (
        jnp.zeros((2, sub_rows, channels), jnp.float32),
        jnp.zeros((2, sub_rows, channels), jnp.float32),
        jnp.zeros((2, channels), jnp.float32),
    )
    shard_part = lax.all_gather(product[None], "ctx", axis=0, tiled=True)

    def visit_member(member, state):
        block_data = lax.dynamic_index_in_dim(shard_part, member, 0, keepdims=False).reshape(
            2, sub_rows, channels
        )
        source_real, source_imag, source_nyquist = spectrum(block_data)
        return add_term(state, source_real, source_imag, source_nyquist, member)

    totals = lax.fori_loop(0, shard_part.shape[0], visit_member, initial)
    halves = []
    for target in range(2):
        halves.append(
            exact_dot(cos_back, totals[0][target])
            - exact_dot(sin_back, totals[1][target])
            + nyquist_back[:, None] * totals[2][target][None, :]
        )
    convolved = jnp.concatenate(halves, 0) / dft_length
    return (gate_branch * (convolved + skip_gain * product_wide)).astype(jnp.bfloat16)


def solution(mesh):
    placed = (P("ctx", "tp"), P(None, None, "tp"), P(None, None, "tp"), P(None, "tp"), P("tp"))
    return jax.shard_map(
        local, mesh=mesh, in_specs=placed, out_specs=P("ctx", "tp"), check_vma=False
    )
```

profile of v0, /device:TPU:1, one launch (start us, length us, event | category | flops | bytes accessed | tf_op | source)
XLA Modules:
  0.0 261.4 jit_solution(9611068512065455228)
XLA Ops:
  7.3 17.0 %copy.8 = bf16[4096,3,512]{0,2,1:T(8,128)(2,1)} copy(bf16[4096,3,512]{2,0,1:T(8,128)(2,1)} %param.8) | data formatting | bytes 25165824 | tf_op args[1]
  24.3 22.3 %all-gather.4.cloned.1.call-done = bf16[128,4096]{1,0:T(8,128)(2,1)} async-done(((bf16[128,512]{1,0:T(8,128)(2,1)}), bf16[128,4096]{1,0:T(8,128)(2,1)}) %all-gather.4.cloned.1.call-update) | async-done | bytes 1048592 | tf_op jit(solution)/shard_map/all_gather | solution.py:31
  46.7 9.2 %convolution_convert_fusion = bf16[128,1536]{1,0:T(8,128)(2,1)S(1)} fusion(bf16[128,4096]{1,0:T(8,128)(2,1)} %all-gather.4.cloned.1.call-done, bf16[4096,1536]{0,1:T(8,128)(2,1)} %bitcast.142), kind=kOutput, calls=%fused_computation.99 | convolution fusion | flops 1610809344 | bytes 14024704 | tf_op jit(solution)/shard_map/dot_general | solution.py:32
  55.9 8.4 %collective-permute-start = (bf16[6,3,512]{2,0,1:T(8,128)(2,1)S(1)}, bf16[6,3,512]{2,0,1:T(8,128)(2,1)S(1)}, u32[]{:S(2)}, u32[]{:S(2)}) collective-permute-start(bf16[6,3,512]{2,0,1:T(8,128)(2,1)S(1)} %bitcast.148), channel_id=1, source_target_pairs={{0,8},{8,16},{16,24},{24,32},{32,40},{40,48},{48,56},{56,64},{64,7... | collective-permute-start | bytes 55304 | tf_op jit(solution)/shard_map/ppermute | solution.py:14
  69.6 2.6 concatenate.16
  73.8 2.6 %concatenate.17 = f32[33,64,512]{2,1,0:T(8,128)} pad(f32[32,64,512]{2,1,0:T(8,128)S(1)} %add_bitcast_fusion, f32[]{:T(128)} %constant.212.clone.1), padding=1_0x0_0x0_0 | pad | bytes 8519684 | tf_op jit(solution)/shard_map/concatenate | solution.py:74
  77.7 39.6 %all-gather.6.cloned.1.call-done = bf16[2048,1,512]{2,0,1:T(8,128)(2,1)} async-done(((bf16[128,1,512]{2,0,1:T(8,128)(2,1)}), bf16[2048,1,512]{2,0,1:T(8,128)(2,1)}) %all-gather.6.cloned.1.call-update) | async-done | bytes 2097168 | tf_op jit(solution)/shard_map/all_gather | solution.py:121
  118.1 130.9 %while.24 = (s32[]{:T(128)}, f32[2,64,512]{2,1,0:T(8,128)S(1)}, f32[2,64,512]{2,1,0:T(8,128)}, f32[2,512]{1,0:T(2,128)S(1)}, s32[]{:T(128)}, /*index=5*/f32[33,6...) while((s32[]{:T(128)}, f32[2,64,512]{2,1,0:T(8,128)S(1)}, ...), condition=%wide.region_1.2_spmd.clone.clone, body=%wide.region_0.1_spmd.clone.clone.sunk | while | flops 36070464 | bytes 9090577 | solution.py:130
  120.2 1.6 multiply_add_fusion.5
  121.8 1.2 multiply_subtract_fusion.3
  123.0 1.4 multiply_add_fusion.6
  128.4 1.6 multiply_add_fusion.5
  129.9 1.2 multiply_subtract_fusion.3
  131.2 1.4 multiply_add_fusion.6
  133.4 1.0 add_add_fusion.2
  136.6 1.6 multiply_add_fusion.5
  138.1 1.2 multiply_subtract_fusion.3
  139.4 1.4 multiply_add_fusion.6
  141.6 1.0 add_add_fusion.2
  144.7 1.6 multiply_add_fusion.5
  146.3 1.2 multiply_subtract_fusion.3
  147.6 1.4 multiply_add_fusion.6
  149.8 1.0 add_add_fusion.2
  152.9 1.6 multiply_add_fusion.5
  154.5 1.2 multiply_subtract_fusion.3
  155.7 1.4 multiply_add_fusion.6
  161.1 1.6 multiply_add_fusion.5
  162.7 1.2 multiply_subtract_fusion.3
  163.9 1.4 multiply_add_fusion.6
  169.3 1.6 multiply_add_fusion.5
  170.9 1.2 multiply_subtract_fusion.3
  172.1 1.4 multiply_add_fusion.6
  177.5 1.6 multiply_add_fusion.5
  179.1 1.2 multiply_subtract_fusion.3
  180.3 1.4 multiply_add_fusion.6
  182.5 1.0 add_add_fusion.2
  185.7 1.6 multiply_add_fusion.5
  187.2 1.2 multiply_subtract_fusion.3
  188.5 1.4 multiply_add_fusion.6
  190.7 1.0 add_add_fusion.2
  193.9 1.6 multiply_add_fusion.5
  195.4 1.2 multiply_subtract_fusion.3
  196.7 1.4 multiply_add_fusion.6
  202.0 1.6 multiply_add_fusion.5
  203.6 1.2 multiply_subtract_fusion.3
  204.9 1.4 multiply_add_fusion.6
  210.2 1.6 multiply_add_fusion.5
  211.8 1.2 multiply_subtract_fusion.3
  213.0 1.4 multiply_add_fusion.6
  218.4 1.6 multiply_add_fusion.5
  220.0 1.2 multiply_subtract_fusion.3
  221.2 1.4 multiply_add_fusion.6
  226.6 1.6 multiply_add_fusion.5
  228.2 1.2 multiply_subtract_fusion.3
  229.4 1.4 multiply_add_fusion.6
  234.8 1.6 multiply_add_fusion.5
  236.4 1.2 multiply_subtract_fusion.3
  237.6 1.4 multiply_add_fusion.6
  243.0 1.6 multiply_add_fusion.5
  244.5 1.2 multiply_subtract_fusion.3
  245.8 1.4 multiply_add_fusion.6
  249.9 1.3 fusion.77
  251.3 1.4 fusion.78
  252.6 1.9 fusion.87
  (208 shorter events, 68.4 us)
Async XLA Ops:
  6.5 61.1 %copy-start = (bf16[2048,512]{1,0:T(8,128)(2,1)S(1)}, bf16[2048,512]{1,0:T(8,128)(2,1)}, u32[]{:S(2)}) copy-start(bf16[2048,512]{1,0:T(8,128)(2,1)} %param.10) | copy-start | bytes 6291460
  6.5 40.1 %all-gather.4.cloned.1.call-start = ((), (), s32[]{:S(2)}) async-start(), calls=%async_computation | async-start | bytes 1179648 | tf_op jit(solution)/shard_map/all_gather | solution.py:31
  7.3 17.0 %copy-start.2 = (f32[7,3,512]{2,0,1:T(8,128)S(1)}, f32[7,3,512]{2,0,1:T(8,128)}, u32[]{:S(2)}) copy-start(f32[7,3,512]{2,0,1:T(8,128)} %param.9) | copy-start | bytes 129028
  7.3 110.1 %all-gather.6.cloned.1.call-start = ((), (), s32[]{:S(2)}) async-start(), calls=%async_computation.1 | async-start | bytes 2228224 | tf_op jit(solution)/shard_map/all_gather | solution.py:121
  55.9 9.4 %collective-permute-start = (bf16[6,3,512]{2,0,1:T(8,128)(2,1)S(1)}, bf16[6,3,512]{2,0,1:T(8,128)(2,1)S(1)}, u32[]{:S(2)}, u32[]{:S(2)}) collective-permute-start(bf16[6,3,512]{2,0,1:T(8,128)(2,1)S(1)} %bitcast.148), channel_id=1, source_target_pairs={{0,8},{8,16},{16,24},{24,32},{32,40},{40,48},{48,56},{56,64},{64,7... | collective-permute-start | bytes 55304 | tf_op jit(solution)/shard_map/ppermute | solution.py:14
  66.0 0.9 copy-start.1
Sparse Core Ops, SparseCore 0:
  9.0 37.5 all-gather.3
  67.7 49.5 all-gather.5
where the time goes:
time: 264 us; the launch traced here: 261 us
  other arithmetic  97.9 us (37%)
  waiting for transfers between devices  63.2 us (24%)
  local copies, waits for them, and re-layouts  39.7 us (15%)
  matrix products  36.7 us (14%)
  between operations  13.6 us (5%)
  starting transfers between devices  8.48 us (3%)
    add x32, other arithmetic, add_term(): total_imag + gain_real * source_imag[half] + gain_imag * source_real[half]  46.9 us
    all_gather x1, waiting for transfers between devices, local(): shard_part = lax.all_gather(product[None], 'ctx', axis=0, tiled=True)  39.6 us
    all_gather x1, waiting for transfers between devices, local(): gathered = lax.all_gather(tokens, 'tp', axis=1, tiled=True)  22.3 us
    sub x16, other arithmetic, add_term(): total_real + gain_real * source_real[half] - gain_imag * source_imag[half]  19.5 us
    unnamed x11, local copies, waits for them, and re-layouts  17.9 us
    add x16, other arithmetic, add_term(): total_nyquist = total_nyquist + gain_nyquist * source_nyquist[half]  15.4 us
    dynamic_slice x16, local copies, waits for them, and re-layouts, visit_member(): lax.dynamic_index_in_dim(shard_part, member, 0, keepdims=False)  14.7 us
    another operation x32, other arithmetic, add_term(): return (jnp.stack(next_real), jnp.stack(next_imag), jnp.stack(next_nyquist))  12 us
  transfers between devices with their start and end apart: 3, of which 3 were waited for; matrix products, arithmetic and copies ran while one was open for 11% of the time, Pallas kernels for 0%

commit v1 on v0

v1 whole, which is shorter than its diff:
```python
import functools

import jax
import jax.numpy as jnp
import ml_dtypes
import numpy as np
from jax import lax
from jax.experimental import pallas as pl
from jax.experimental.pallas import tpu as pltpu
from jax.sharding import PartitionSpec as P

TAPS = 7
MESH = pl.DeviceIdType.MESH
ROWS = 128
HALO = 8
PAD = 16
DEPTH = 512
CH = 512
NCTX = 16
NZ = 4
PART = CH // NCTX
SUB = 32
F32 = jnp.float32
BF16 = jnp.bfloat16


def split(table):
    high = table.astype(ml_dtypes.bfloat16)
    low = (table - high.astype(np.float64)).astype(ml_dtypes.bfloat16)
    return high, low


def tables():
    size = 2 * ROWS
    time = np.arange(ROWS)[:, None]
    freq = np.arange(ROWS)[None, :]
    angle = 2 * np.pi * (time * freq % size) / size
    imag = -np.sin(angle)
    imag[:, 0] = np.where(np.arange(ROWS) % 2 == 0, 1.0, -1.0)
    forward = np.concatenate([np.cos(angle), imag], 1)
    weight = np.where(np.arange(ROWS) == 0, 1.0, 2.0)[None, :] / size
    back_real = np.cos(angle) * weight
    back_imag = -np.sin(angle) * weight
    back_imag[:, 0] = np.where(np.arange(ROWS) % 2 == 0, 1.0, -1.0) / size
    inverse = np.concatenate([back_real, back_imag], 1).T
    return (*split(forward), *split(inverse))


def nt_dot(left, right):
    return lax.dot_general(left, right, (((1,), (1,)), ((), ())), preferred_element_type=F32)


def dot(left, right):
    return jnp.dot(left, right, preferred_element_type=F32)


def eye(rows, columns, offset):
    row = lax.broadcasted_iota(jnp.int32, (rows, columns), 0)
    column = lax.broadcasted_iota(jnp.int32, (rows, columns), 1)
    return row + offset == column


def kernel(
    tokens, weight, taps, filters, skip, fwd_hi, fwd_lo, inv_hi, inv_lo, out,
    slots, w_v, taps_v, filt_v, skip_v, fh_v, fl_v, ih_v, il_v,
    total, ext, gate, filt_t, spec, gain_re, gain_im, gain_ny, psend, precv, yhat, ysend, yrecv,
    w_sem, load_sem, own_sem, g_send, g_recv, h_send, h_recv, p_send, p_recv, y_send, y_recv,
):
    ctx = lax.axis_index("ctx")
    tp = lax.axis_index("tp")
    y, z = tp // NZ, tp % NZ
    y_side = (1 - y) * NZ + z
    z_up = y * NZ + (z + 1) % NZ
    z_down = y * NZ + (z + NZ - 1) % NZ

    def peer(mask):
        other = ctx
        for bit in (1, 2, 4, 8):
            if mask & bit:
                other = other + bit * (1 - 2 * ((ctx // bit) % 2))
        return other

    for index in range(2 * NZ):
        slots[index, pl.ds(0, PAD)] = jnp.zeros((PAD, DEPTH), BF16)

    barrier = pltpu.get_barrier_semaphore()
    for side in (y_side, z_up, z_down):
        pl.semaphore_signal(barrier, inc=1, device_id={"ctx": ctx, "tp": side}, device_id_type=MESH)
    for mask in range(1, NCTX):
        pl.semaphore_signal(barrier, inc=1, device_id={"ctx": peer(mask), "tp": tp}, device_id_type=MESH)

    loads = [
        pltpu.make_async_copy(src, dst, load_sem.at[index])
        for index, (src, dst) in enumerate(
            [
                (filters.at[:, pl.ds(pl.multiple_of(ctx // 4 * 128, 128), 128)], filt_v),
                (fwd_hi, fh_v),
                (fwd_lo, fl_v),
                (inv_hi, ih_v),
                (inv_lo, il_v),
                (taps, taps_v),
                (skip, skip_v),
            ]
        )
    ]
    own = pltpu.make_async_copy(tokens, slots.at[0, pl.ds(PAD, ROWS)], own_sem.at[0])
    own.start()
    for load in loads:
        load.start()

    def source(dy, dz):
        there = (1 - y) if dy else y
        return there * NZ + (z + dz) % NZ

    def weight_load(dy, dz):
        rows = pl.ds(pl.multiple_of(source(dy, dz) * DEPTH, DEPTH), DEPTH)
        return pltpu.make_async_copy(weight.at[:, rows], w_v.at[:, rows], w_sem.at[dy * NZ + dz])

    order = [(0, 0), (1, 0), (0, 3), (0, 1), (0, 2), (1, 3), (1, 1), (1, 2)]
    for dy, dz in order:
        weight_load(dy, dz).start()

    pl.semaphore_wait(barrier, 3 + NCTX - 1)

    def rows_of(piece):
        return pl.ds(PAD + piece * SUB, SUB)

    pieces = ROWS // SUB
    low = list(range(pieces // 2))
    high = list(range(pieces // 2, pieces))

    def gather_copy(src_slot, piece, dst_slot, side):
        first = src_slot == (0, 0)
        src = tokens.at[pl.ds(piece * SUB, SUB)] if first else slots.at[src_slot[0] * NZ + src_slot[1], rows_of(piece)]
        index = dst_slot[0] * NZ + dst_slot[1]
        return pltpu.make_async_remote_copy(
            src_ref=src,
            dst_ref=slots.at[index, rows_of(piece)],
            send_sem=g_send.at[index, piece],
            recv_sem=g_recv.at[index, piece],
            device_id={"ctx": ctx, "tp": side},
            device_id_type=MESH,
        )

    sent = []

    def send(src_slot, piece, dst_slot, side):
        copy = gather_copy(src_slot, piece, dst_slot, side)
        copy.start()
        sent.append(copy)

    def arrived(slot, piece):
        gather_copy((1, 1), piece, slot, z_up).wait_recv()

    halo_rows = pl.ds(PAD - HALO, HALO)

    def halo_copy(src_slot, dst_slot, device):
        index = dst_slot[0] * NZ + dst_slot[1]
        src = slots.at[src_slot[0] * NZ + src_slot[1], halo_rows]
        if dst_slot == (0, 0):
            src = tokens.at[pl.ds(ROWS - HALO, HALO)]
        return pltpu.make_async_remote_copy(
            src_ref=src,
            dst_ref=slots.at[index, halo_rows],
            send_sem=h_send.at[index],
            recv_sem=h_recv.at[index],
            device_id=device,
            device_id_type=MESH,
        )

    @pl.when(ctx < NCTX - 1)
    def _():
        halo_copy((0, 0), (0, 0), {"ctx": ctx + 1, "tp": tp}).start()

    for a, b in zip(high, low):
        send((0, 0), a, (1, 0), y_side)
        send((0, 0), a, (0, 3), z_up)
        send((0, 0), b, (0, 1), z_down)
        send((0, 0), b, (1, 0), y_side)
    for a, b in zip(high, low):
        send((0, 0), b, (0, 3), z_up)
        send((0, 0), a, (0, 1), z_down)

    halo_hops = [
        ((0, 0), (1, 0), y_side),
        ((0, 0), (0, 3), z_up),
        ((0, 0), (0, 1), z_down),
        ((0, 3), (0, 2), z_up),
        ((1, 0), (1, 3), z_up),
        ((1, 0), (1, 1), z_down),
        ((1, 3), (1, 2), z_up),
    ]

    def halo_arrived(slot):
        halo_copy((0, 1), slot, {"ctx": ctx, "tp": z_up}).wait_recv()

    def halo_from(slot):
        for src, dst, side in halo_hops:
            if src == slot:
                halo_copy(src, dst, {"ctx": ctx, "tp": side}).start()

    def halo_step(slot):
        @pl.when(ctx > 0)
        def _():
            halo_arrived(slot)
            halo_from(slot)

    for load in loads:
        load.wait()
    pick = eye(PART, 128, ctx % 4 * PART)
    across = nt_dot(pick.astype(BF16), filt_v[...]).astype(BF16)
    for block in range(NCTX):
        filt_t[pl.ds(block * PART, PART)] = across[:, block * ROWS : (block + 1) * ROWS]
    spec[...] = dot(filt_t[...], fh_v[...]) + dot(filt_t[...], fl_v[...])
    lane = lax.broadcasted_iota(jnp.int32, (PART, ROWS), 1)
    swap = jnp.where(lane % 2 == 0, 1.0, -1.0).astype(F32)
    first_lane = lane == 0
    for block in range(NCTX):
        now = pl.ds(block * PART, PART)
        real = spec[now, :ROWS]
        imag = spec[now, ROWS:]
        if block:
            before = pl.ds((block - 1) * PART, PART)
            real = real + swap * spec[before, :ROWS]
            imag = imag + swap * spec[before, ROWS:]
        gain_re[now] = real
        gain_im[now] = jnp.where(first_lane, 0.0, imag)
        gain_ny[now] = jnp.where(first_lane, imag, real)

    own.wait()
    halo_step((0, 0))

    def project(slot, start):
        weight_load(*slot).wait()
        index = slot[0] * NZ + slot[1]
        rows = pl.ds(pl.multiple_of(source(*slot) * DEPTH, DEPTH), DEPTH)

        def branch(b, carry):
            term = dot(slots[index], w_v[b, rows])
            total[b] = term if start else total[b] + term
            return carry

        lax.fori_loop(0, 3, branch, 0)

    project((0, 0), True)

    for a, b in zip(high, low):
        arrived((1, 0), a)
        send((1, 0), a, (1, 3), z_up)
        arrived((0, 1), b)
        send((0, 1), b, (0, 2), z_down)
        arrived((0, 3), a)
        send((0, 3), a, (0, 2), z_up)
        arrived((1, 0), b)
        send((1, 0), b, (1, 1), z_down)
    halo_step((1, 0))
    project((1, 0), False)
    for a, b in zip(high, low):
        arrived((0, 3), b)
        send((0, 3), b, (1, 3), y_side)
        arrived((0, 1), a)
        send((0, 1), a, (1, 1), y_side)
    halo_step((0, 3))
    halo_step((0, 1))
    project((0, 3), False)
    for a, b in zip(high, low):
        arrived((1, 3), a)
        send((1, 3), a, (1, 2), z_up)
        arrived((1, 1), b)
        send((1, 1), b, (1, 2), z_down)
    halo_step((1, 3))
    project((0, 1), False)
    for piece in range(pieces):
        arrived((0, 2), piece)
    halo_step((0, 2))
    project((0, 2), False)
    for piece in low:
        arrived((1, 3), piece)
    project((1, 3), False)
    for piece in high:
        arrived((1, 1), piece)
    halo_step((1, 1))
    project((1, 1), False)
    for piece in range(pieces):
        arrived((1, 2), piece)
    halo_step((1, 2))
    project((1, 2), False)

    ident = eye(ROWS, ROWS, 0).astype(BF16)
    for group in range(CH // 128):
        lanes = slice(group * 128, (group + 1) * 128)
        branches = []
        for b in range(3):
            ext[b] = total[b, :, lanes].astype(BF16).astype(F32)
            acc = taps_v[b, 0:1, lanes] * ext[b, pl.ds(PAD - TAPS + 1, ROWS)]
            for t in range(1, TAPS):
                acc = acc + taps_v[b, t : t + 1, lanes] * ext[b, pl.ds(PAD - TAPS + 1 + t, ROWS)]
            branches.append(acc)
        gate[:, lanes] = branches[0]
        product = (branches[1] * branches[2]).astype(BF16)
        turned = nt_dot(ident, product).astype(BF16)
        for part in range(128 // PART):
            psend[group * (128 // PART) + part] = turned[part * PART : (part + 1) * PART]

    far_first = [12, 13, 10, 11, 14, 15, 8, 9, 4, 5, 2, 3, 6, 7, 1]

    def exchange(send_buffer, recv_buffer, send_sem, recv_sem):
        copies = []
        for mask in far_first:
            other = peer(mask)
            copy = pltpu.make_async_remote_copy(
                src_ref=send_buffer.at[other],
                dst_ref=recv_buffer.at[ctx],
                send_sem=send_sem.at[mask],
                recv_sem=recv_sem.at[mask],
                device_id={"ctx": other, "tp": tp},
                device_id_type=MESH,
            )
            copy.start()
            copies.append(copy)
        recv_buffer[pl.ds(ctx, 1)] = send_buffer[pl.ds(ctx, 1)]
        for copy in copies:
            copy.wait()

    exchange(psend, precv, p_send, p_recv)

    block_rows = precv[...].reshape(NCTX * PART, ROWS)
    spec[...] = dot(block_rows, fh_v[...]) + dot(block_rows, fl_v[...])
    for block in range(NCTX):
        real = jnp.zeros((PART, ROWS), F32)
        imag = jnp.zeros((PART, ROWS), F32)
        for earlier in range(block + 1):
            lag = pl.ds((block - earlier) * PART, PART)
            src = pl.ds(earlier * PART, PART)
            p_real = spec[src, :ROWS]
            p_imag = spec[src, ROWS:]
            cross = gain_im[lag]
            real = real + gain_re[lag] * p_real - cross * p_imag
            imag = imag + gain_ny[lag] * p_imag + cross * p_real
        now = pl.ds(block * PART, PART)
        yhat[now, :ROWS] = real
        yhat[now, ROWS:] = imag
    both = yhat[...]
    upper = both.astype(BF16)
    lower = (both - upper.astype(F32)).astype(BF16)
    convolved = dot(upper, ih_v[...]) + dot(upper, il_v[...]) + dot(lower, ih_v[...])
    skip_row = skip_v[:, pl.ds(pl.multiple_of(ctx // 4 * 128, 128), 128)]
    skip_column = jnp.sum(jnp.where(pick, skip_row, 0.0), axis=1, keepdims=True)
    direct = skip_column[None] * precv[...].astype(F32)
    ysend[...] = (convolved.reshape(NCTX, PART, ROWS) + direct).astype(BF16)

    exchange(ysend, yrecv, y_send, y_recv)

    mixed = nt_dot(ident, yrecv[...].reshape(CH, ROWS))
    out[...] = (gate[...] * mixed).astype(BF16)

    for copy in sent:
        copy.wait_send()

    @pl.when(ctx < NCTX - 1)
    def _():
        halo_copy((0, 0), (0, 0), {"ctx": ctx + 1, "tp": tp}).wait_send()

    @pl.when(ctx > 0)
    def _():
        for src, dst, side in halo_hops:
            halo_copy(src, dst, {"ctx": ctx, "tp": side}).wait_send()


def local(tokens, in_weight, conv_weight, filters, skip_gain):
    any_space = pl.BlockSpec(memory_space=pl.ANY)
    dma = pltpu.SemaphoreType.DMA
    pieces = ROWS // SUB
    size = 2 * ROWS
    scratch = [
        pltpu.VMEM((2 * NZ, PAD + ROWS, DEPTH), BF16),
        pltpu.VMEM((3, 2 * NZ * DEPTH, CH), BF16),
        pltpu.VMEM((3, TAPS, CH), F32),
        pltpu.VMEM((NCTX * ROWS, 128), BF16),
        pltpu.VMEM((1, CH), F32),
        pltpu.VMEM((ROWS, size), BF16),
        pltpu.VMEM((ROWS, size), BF16),
        pltpu.VMEM((size, ROWS), BF16),
        pltpu.VMEM((size, ROWS), BF16),
        pltpu.VMEM((3, PAD + ROWS, CH), F32),
        pltpu.VMEM((3, PAD + ROWS, 128), F32),
        pltpu.VMEM((ROWS, CH), F32),
        pltpu.VMEM((NCTX * PART, ROWS), BF16),
        pltpu.VMEM((NCTX * PART, size), F32),
        pltpu.VMEM((NCTX * PART, ROWS), F32),
        pltpu.VMEM((NCTX * PART, ROWS), F32),
        pltpu.VMEM((NCTX * PART, ROWS), F32),
        pltpu.VMEM((NCTX, PART, ROWS), BF16),
        pltpu.VMEM((NCTX, PART, ROWS), BF16),
        pltpu.VMEM((NCTX * PART, size), F32),
        pltpu.VMEM((NCTX, PART, ROWS), BF16),
        pltpu.VMEM((NCTX, PART, ROWS), BF16),
        dma((2 * NZ,)),
        dma((7,)),
        dma((1,)),
        dma((2 * NZ, pieces)),
        dma((2 * NZ, pieces)),
        dma((2 * NZ,)),
        dma((2 * NZ,)),
        dma((NCTX,)),
        dma((NCTX,)),
        dma((NCTX,)),
        dma((NCTX,)),
    ]
    return pl.pallas_call(
        kernel,
        out_shape=jax.ShapeDtypeStruct((ROWS, CH), BF16),
        in_specs=[any_space] * 9,
        out_specs=pl.BlockSpec(memory_space=pltpu.VMEM),
        scratch_shapes=scratch,
        compiler_params=pltpu.CompilerParams(
            collective_id=0, has_side_effects=True, vmem_limit_bytes=56 * 1024 * 1024
        ),
        name="hyena",
    )(
        tokens,
        jnp.transpose(in_weight, (1, 0, 2)),
        jnp.transpose(conv_weight, (1, 0, 2)),
        filters,
        skip_gain.reshape(1, CH),
        *(jnp.asarray(table) for table in tables()),
    )


def solution(mesh):
    placed = (P("ctx", "tp"), P(None, None, "tp"), P(None, None, "tp"), P(None, "tp"), P("tp"))
    return jax.shard_map(local, mesh=mesh, in_specs=placed, out_specs=P("ctx", "tp"), check_vma=False)
```

time: 264 us -> 37.6 us (0.14)
  other arithmetic: 97.9 us -> 0 us
  waiting for transfers between devices: 63.2 us -> 0 us
  local copies, waits for them, and re-layouts: 39.7 us -> 1.57 us
  matrix products: 36.7 us -> 0 us
  Pallas kernels: 0 us -> 35.9 us
  between operations: 13.6 us -> 0.01 us
  starting transfers between devices: 8.48 us -> 0 us
    add x50 -> x0, other arithmetic: 63 us -> none  [the longest x32 46.9 us: add_term(): total_imag + gain_real * source_imag[half] + gain_imag * source_real[half]]
    all_gather x2 -> x0, waiting for transfers between devices: 62 us -> none  [the longest x1 39.6 us: local(): shard_part = lax.all_gather(product[None], 'ctx', axis=0, tiled=True)]
    dot_general x90 -> x0, matrix products: 36.7 us -> none  [the longest x1 9.18 us: local(): summed = jnp.dot(gathered, flat_weight, preferred_element_type=jnp.float32)]
    pallas_call x0 -> x1, Pallas kernels: none -> 35.9 us  [local(): pl.pallas_call(kernel, out_shape=jax.ShapeDtypeStruct((ROWS, CH), BF16),...]
    sub x16 -> x0, other arithmetic: 19.5 us -> none  [add_term(): total_real + gain_real * source_real[half] - gain_imag * source_imag[half]]
    unnamed x11 -> x1, local copies, waits for them, and re-layouts: 17.9 us -> 1.57 us
    dynamic_slice x16 -> x0, local copies, waits for them, and re-layouts: 14.7 us -> none  [visit_member(): lax.dynamic_index_in_dim(shard_part, member, 0, keepdims=False)]
    another operation x32 -> x0, other arithmetic: 12 us -> none  [add_term(): return (jnp.stack(next_real), jnp.stack(next_imag), jnp.stack(next_nyquist))]
  transfers between devices with their start and end apart: 3 -> 0, of which waited for: 3 -> 0; matrix products, arithmetic and copies ran while one was open for 11% -> 0% of each run, Pallas kernels for 0% -> 0%
where the time goes in v1:
time: 37.6 us; the launch traced here: 37.5 us
  Pallas kernels  35.9 us (95%)
  local copies, waits for them, and re-layouts  1.57 us (4%)
    pallas_call x1, Pallas kernels, local(): pl.pallas_call(kernel, out_shape=jax.ShapeDtypeStruct((ROWS, CH), BF16),...  35.9 us
    unnamed x1, local copies, waits for them, and re-layouts  1.57 us

profile of v1, /device:TPU:1, one launch (start us, length us, event | category | flops | bytes accessed | tf_op | source)
XLA Modules:
  0.0 37.5 jit_solution(12316164174427218331)
XLA Ops:
  0.0 35.9 %hyena.1 = bf16[128,512]{1,0:T(8,128)(2,1)} custom-call(bf16[128,512]{1,0:T(8,128)(2,1)} %tokens.1, bf16[3,4096,512]{2,1,0:T(8,128)(2,1)} %bitcast.3, f32[3,7,512]{2,1,0:T(8,128)} %bitcast.4, bf16[2048,512]{1,0:T(8,128)(2,1)} %filters.1, f32[1,512]{1,0:T(1,128)} %bitcast.5, bf16[128,256]{1,0:T(8,128)(2,1)} %constant.8.clone.fwd_hi, ...), custom_call_target="tpu_custom_call" | custom-call | tf_op jit(solution)/shard_map/hyena/pallas_call | solution.py:410
  35.9 1.6 %copy.11 = bf16[128,512]{1,0:T(8,128)(2,1)} copy(bf16[128,512]{1,0:T(8,128)(2,1)} %hyena.1) | data formatting | bytes 262144

commit v2 on v1

--- a/solution.py
+++ b/solution.py
@@ -64,7 +64,7 @@
     tokens, weight, taps, filters, skip, fwd_hi, fwd_lo, inv_hi, inv_lo, out,
     slots, w_v, taps_v, filt_v, skip_v, fh_v, fl_v, ih_v, il_v,
     total, ext, gate, filt_t, spec, gain_re, gain_im, gain_ny, psend, precv, yhat, ysend, yrecv,
-    w_sem, load_sem, own_sem, g_send, g_recv, h_send, h_recv, p_send, p_recv, y_send, y_recv,
+    w_sem, load_sem, own_sem, g_send, g_recv, h_send, h_recv, p_send, p_recv, y_send, y_recv, ready,
 ):
     ctx = lax.axis_index("ctx")
     tp = lax.axis_index("tp")
@@ -86,8 +86,17 @@
     barrier = pltpu.get_barrier_semaphore()
     for side in (y_side, z_up, z_down):
         pl.semaphore_signal(barrier, inc=1, device_id={"ctx": ctx, "tp": side}, device_id_type=MESH)
-    for mask in range(1, NCTX):
-        pl.semaphore_signal(barrier, inc=1, device_id={"ctx": peer(mask), "tp": tp}, device_id_type=MESH)
+    beside = (ctx + jnp.where(ctx % 2 == 0, NCTX - 1, 1)) % NCTX
+    for other in (peer(1), peer(2), peer(4), peer(8), beside):
+        pl.semaphore_signal(barrier, inc=1, device_id={"ctx": other, "tp": tp}, device_id_type=MESH)
+
+    def tell(turn):
+        pl.semaphore_signal(
+            ready.at[turn], inc=1, device_id={"ctx": peer(1 << turn), "tp": tp}, device_id_type=MESH
+        )
+
+    def hear(turn):
+        pl.semaphore_wait(ready.at[turn], 1)
 
     loads = [
         pltpu.make_async_copy(src, dst, load_sem.at[index])
@@ -120,7 +129,7 @@
     for dy, dz in order:
         weight_load(dy, dz).start()
 
-    pl.semaphore_wait(barrier, 3 + NCTX - 1)
+    pl.semaphore_wait(barrier, 8)
 
     def rows_of(piece):
         return pl.ds(PAD + piece * SUB, SUB)
@@ -204,6 +213,8 @@
         def _():
             halo_arrived(slot)
             halo_from(slot)
+
+    tell(0)
 
     for load in loads:
         load.wait()
@@ -242,6 +253,8 @@
 
         lax.fori_loop(0, 3, branch, 0)
 
+    hear(0)
+    tell(1)
     project((0, 0), True)
 
     for a, b in zip(high, low):
@@ -253,6 +266,8 @@
         send((0, 3), a, (0, 2), z_up)
         arrived((1, 0), b)
         send((1, 0), b, (1, 1), z_down)
+    hear(1)
+    tell(2)
     halo_step((1, 0))
     project((1, 0), False)
     for a, b in zip(high, low):
@@ -286,43 +301,43 @@
     halo_step((1, 2))
     project((1, 2), False)
 
+    hear(2)
+
+    def message(send_buffer, recv_buffer, send_sem, recv_sem, mask):
+        other = peer(mask)
+        copy = pltpu.make_async_remote_copy(
+            src_ref=send_buffer.at[other],
+            dst_ref=recv_buffer.at[ctx],
+            send_sem=send_sem.at[mask],
+            recv_sem=recv_sem.at[mask],
+            device_id={"ctx": other, "tp": tp},
+            device_id_type=MESH,
+        )
+        copy.start()
+        return copy
+
     ident = eye(ROWS, ROWS, 0).astype(BF16)
-    for group in range(CH // 128):
-        lanes = slice(group * 128, (group + 1) * 128)
+    per = 128 // PART
+    copies = []
+    for far, near in ((3, (0, 1, 2, 3)), (2, (2, 3, 0, 1)), (1, (0, 1, 2, 3)), (0, (2, 3, 1))):
+        quad = peer(far * per) // per
+        lanes = pl.ds(pl.multiple_of(quad * 128, 128), 128)
         branches = []
         for b in range(3):
             ext[b] = total[b, :, lanes].astype(BF16).astype(F32)
-            acc = taps_v[b, 0:1, lanes] * ext[b, pl.ds(PAD - TAPS + 1, ROWS)]
+            acc = taps_v[b, pl.ds(0, 1), lanes] * ext[b, pl.ds(PAD - TAPS + 1, ROWS)]
             for t in range(1, TAPS):
-                acc = acc + taps_v[b, t : t + 1, lanes] * ext[b, pl.ds(PAD - TAPS + 1 + t, ROWS)]
+                acc = acc + taps_v[b, pl.ds(t, 1), lanes] * ext[b, pl.ds(PAD - TAPS + 1 + t, ROWS)]
             branches.append(acc)
         gate[:, lanes] = branches[0]
         product = (branches[1] * branches[2]).astype(BF16)
         turned = nt_dot(ident, product).astype(BF16)
-        for part in range(128 // PART):
-            psend[group * (128 // PART) + part] = turned[part * PART : (part + 1) * PART]
-
-    far_first = [12, 13, 10, 11, 14, 15, 8, 9, 4, 5, 2, 3, 6, 7, 1]
-
-    def exchange(send_buffer, recv_buffer, send_sem, recv_sem):
-        copies = []
-        for mask in far_first:
-            other = peer(mask)
-            copy = pltpu.make_async_remote_copy(
-                src_ref=send_buffer.at[other],
-                dst_ref=recv_buffer.at[ctx],
-                send_sem=send_sem.at[mask],
-                recv_sem=recv_sem.at[mask],
-                device_id={"ctx": other, "tp": tp},
-                device_id_type=MESH,
-            )
-            copy.start()
-            copies.append(copy)
-        recv_buffer[pl.ds(ctx, 1)] = send_buffer[pl.ds(ctx, 1)]
-        for copy in copies:
-            copy.wait()
-
-    exchange(psend, precv, p_send, p_recv)
+        psend[pl.ds(quad * per, per)] = turned.reshape(per, PART, ROWS)
+        for low_mask in near:
+            copies.append(message(psend, precv, p_send, p_recv, far * per + low_mask))
+    precv[pl.ds(ctx, 1)] = psend[pl.ds(ctx, 1)]
+    for copy in copies:
+        copy.wait()
 
     block_rows = precv[...].reshape(NCTX * PART, ROWS)
     spec[...] = dot(block_rows, fh_v[...]) + dot(block_rows, fl_v[...])
@@ -349,7 +364,11 @@
     direct = skip_column[None] * precv[...].astype(F32)
     ysend[...] = (convolved.reshape(NCTX, PART, ROWS) + direct).astype(BF16)
 
-    exchange(ysend, yrecv, y_send, y_recv)
+    far_first = [12, 13, 10, 11, 14, 15, 8, 9, 4, 5, 2, 3, 6, 7, 1]
+    copies = [message(ysend, yrecv, y_send, y_recv, mask) for mask in far_first]
+    yrecv[pl.ds(ctx, 1)] = ysend[pl.ds(ctx, 1)]
+    for copy in copies:
+        copy.wait()
 
     mixed = nt_dot(ident, yrecv[...].reshape(CH, ROWS))
     out[...] = (gate[...] * mixed).astype(BF16)
@@ -406,6 +425,7 @@
         dma((NCTX,)),
         dma((NCTX,)),
         dma((NCTX,)),
+        pltpu.SemaphoreType.REGULAR((3,)),
     ]
     return pl.pallas_call(
         kernel,

time: 37.6 us -> 36.2 us (0.963)
  Pallas kernels: 35.9 us -> 34.5 us
    pallas_call x1, Pallas kernels: 35.9 us -> 34.5 us  [local(): pl.pallas_call(kernel, out_shape=jax.ShapeDtypeStruct((ROWS, CH), BF16),...]
where the time goes in v2:
time: 36.2 us; the launch traced here: 36 us
  Pallas kernels  34.5 us (95%)
  local copies, waits for them, and re-layouts  1.57 us (4%)
    pallas_call x1, Pallas kernels, local(): pl.pallas_call(kernel, out_shape=jax.ShapeDtypeStruct((ROWS, CH), BF16),...  34.5 us
    unnamed x1, local copies, waits for them, and re-layouts  1.57 us

profile of v2, /device:TPU:1, one launch (start us, length us, event | category | flops | bytes accessed | tf_op | source)
XLA Modules:
  0.0 36.0 jit_solution(16402284492937904705)
XLA Ops:
  0.0 34.5 %hyena.1 = bf16[128,512]{1,0:T(8,128)(2,1)} custom-call(bf16[128,512]{1,0:T(8,128)(2,1)} %tokens.1, bf16[3,4096,512]{2,1,0:T(8,128)(2,1)} %bitcast.3, f32[3,7,512]{2,1,0:T(8,128)} %bitcast.4, bf16[2048,512]{1,0:T(8,128)(2,1)} %filters.1, f32[1,512]{1,0:T(1,128)} %bitcast.5, bf16[128,256]{1,0:T(8,128)(2,1)} %constant.8.clone.fwd_hi, ...), custom_call_target="tpu_custom_call" | custom-call | tf_op jit(solution)/shard_map/hyena/pallas_call | solution.py:430
  34.5 1.6 %copy.11 = bf16[128,512]{1,0:T(8,128)(2,1)} copy(bf16[128,512]{1,0:T(8,128)(2,1)} %hyena.1) | data formatting | bytes 262144

commit v3 on v2

--- a/solution.py
+++ b/solution.py
@@ -305,7 +305,7 @@
 
     def message(send_buffer, recv_buffer, send_sem, recv_sem, mask):
         other = peer(mask)
-        copy = pltpu.make_async_remote_copy(
+        return pltpu.make_async_remote_copy(
             src_ref=send_buffer.at[other],
             dst_ref=recv_buffer.at[ctx],
             send_sem=send_sem.at[mask],
@@ -313,12 +313,15 @@
             device_id={"ctx": other, "tp": tp},
             device_id_type=MESH,
         )
-        copy.start()
-        return copy
+
+    def p_message(mask):
+        return message(psend, precv, p_send, p_recv, mask)
+
+    def y_message(mask):
+        return message(ysend, yrecv, y_send, y_recv, mask)
 
     ident = eye(ROWS, ROWS, 0).astype(BF16)
     per = 128 // PART
-    copies = []
     for far, near in ((3, (0, 1, 2, 3)), (2, (2, 3, 0, 1)), (1, (0, 1, 2, 3)), (0, (2, 3, 1))):
         quad = peer(far * per) // per
         lanes = pl.ds(pl.multiple_of(quad * 128, 128), 128)
@@ -334,45 +337,94 @@
         turned = nt_dot(ident, product).astype(BF16)
         psend[pl.ds(quad * per, per)] = turned.reshape(per, PART, ROWS)
         for low_mask in near:
-            copies.append(message(psend, precv, p_send, p_recv, far * per + low_mask))
+            p_message(far * per + low_mask).start()
     precv[pl.ds(ctx, 1)] = psend[pl.ds(ctx, 1)]
-    for copy in copies:
-        copy.wait()
-
-    block_rows = precv[...].reshape(NCTX * PART, ROWS)
-    spec[...] = dot(block_rows, fh_v[...]) + dot(block_rows, fl_v[...])
-    for block in range(NCTX):
-        real = jnp.zeros((PART, ROWS), F32)
-        imag = jnp.zeros((PART, ROWS), F32)
-        for earlier in range(block + 1):
-            lag = pl.ds((block - earlier) * PART, PART)
-            src = pl.ds(earlier * PART, PART)
-            p_real = spec[src, :ROWS]
-            p_imag = spec[src, ROWS:]
-            cross = gain_im[lag]
-            real = real + gain_re[lag] * p_real - cross * p_imag
-            imag = imag + gain_ny[lag] * p_imag + cross * p_real
-        now = pl.ds(block * PART, PART)
-        yhat[now, :ROWS] = real
-        yhat[now, ROWS:] = imag
-    both = yhat[...]
-    upper = both.astype(BF16)
-    lower = (both - upper.astype(F32)).astype(BF16)
-    convolved = dot(upper, ih_v[...]) + dot(upper, il_v[...]) + dot(lower, ih_v[...])
+
+    half_blocks = NCTX // 2
+    near_masks = [4, 5, 2, 3, 6, 7, 1]
+    far_masks = [12, 13, 10, 11, 14, 15, 8, 9]
     skip_row = skip_v[:, pl.ds(pl.multiple_of(ctx // 4 * 128, 128), 128)]
     skip_column = jnp.sum(jnp.where(pick, skip_row, 0.0), axis=1, keepdims=True)
-    direct = skip_column[None] * precv[...].astype(F32)
-    ysend[...] = (convolved.reshape(NCTX, PART, ROWS) + direct).astype(BF16)
-
-    far_first = [12, 13, 10, 11, 14, 15, 8, 9, 4, 5, 2, 3, 6, 7, 1]
-    copies = [message(ysend, yrecv, y_send, y_recv, mask) for mask in far_first]
+
+    def blocks_of(half):
+        return pl.ds(half * half_blocks, half_blocks)
+
+    def rows_in(half):
+        return pl.ds(half * half_blocks * PART, half_blocks * PART)
+
+    def forward(half):
+        block_rows = precv[blocks_of(half)].reshape(half_blocks * PART, ROWS)
+        spec[rows_in(half)] = dot(block_rows, fh_v[...]) + dot(block_rows, fl_v[...])
+
+    def gather_terms(to_half, from_half, start):
+        for block in range(to_half * half_blocks, (to_half + 1) * half_blocks):
+            now = pl.ds(block * PART, PART)
+            real = jnp.zeros((PART, ROWS), F32) if start else yhat[now, :ROWS]
+            imag = jnp.zeros((PART, ROWS), F32) if start else yhat[now, ROWS:]
+            for earlier in range(from_half * half_blocks, min(block + 1, (from_half + 1) * half_blocks)):
+                lag = pl.ds((block - earlier) * PART, PART)
+                src = pl.ds(earlier * PART, PART)
+                p_real = spec[src, :ROWS]
+                p_imag = spec[src, ROWS:]
+                cross = gain_im[lag]
+                real = real + gain_re[lag] * p_real - cross * p_imag
+                imag = imag + gain_ny[lag] * p_imag + cross * p_real
+            yhat[now, :ROWS] = real
+            yhat[now, ROWS:] = imag
+
+    def finish(half, masks):
+        both = yhat[rows_in(half)]
+        upper = both.astype(BF16)
+        lower = (both - upper.astype(F32)).astype(BF16)
+        convolved = dot(upper, ih_v[...]) + dot(upper, il_v[...]) + dot(lower, ih_v[...])
+        direct = skip_column[None] * precv[blocks_of(half)].astype(F32)
+        ysend[blocks_of(half)] = (convolved.reshape(half_blocks, PART, ROWS) + direct).astype(BF16)
+        for mask in masks:
+            y_message(mask).start()
+
+    for mask in near_masks:
+        p_message(mask).wait_recv()
+
+    @pl.when(ctx < half_blocks)
+    def _():
+        forward(0)
+        gather_terms(0, 0, True)
+        gather_terms(1, 0, True)
+        for mask in far_masks:
+            p_message(mask).wait_recv()
+        forward(1)
+        gather_terms(1, 1, False)
+        finish(1, far_masks)
+        finish(0, near_masks)
+
+    @pl.when(ctx >= half_blocks)
+    def _():
+        forward(1)
+        gather_terms(1, 1, True)
+        for mask in far_masks:
+            p_message(mask).wait_recv()
+        forward(0)
+        gather_terms(0, 0, True)
+        finish(0, far_masks)
+        gather_terms(1, 0, False)
+        finish(1, near_masks)
+
     yrecv[pl.ds(ctx, 1)] = ysend[pl.ds(ctx, 1)]
-    for copy in copies:
-        copy.wait()
-
-    mixed = nt_dot(ident, yrecv[...].reshape(CH, ROWS))
-    out[...] = (gate[...] * mixed).astype(BF16)
-
+
+    def mix(half, masks):
+        for mask in masks:
+            y_message(mask).wait_recv()
+        lanes = pl.ds(pl.multiple_of(half * (CH // 2), CH // 2), CH // 2)
+        mixed = nt_dot(ident, yrecv[blocks_of(half)].reshape(CH // 2, ROWS))
+        out[:, lanes] = (gate[:, lanes] * mixed).astype(BF16)
+
+    own_half = ctx // half_blocks
+    mix(own_half, near_masks)
+    mix(1 - own_half, far_masks)
+
+    for mask in near_masks + far_masks:
+        p_message(mask).wait_send()
+        y_message(mask).wait_send()
     for copy in sent:
         copy.wait_send()
 

time: 36.2 us -> 35.9 us (level)
  no operation moved by 1% of the time
where the time goes in v3:
time: 35.9 us; the launch traced here: 35.8 us
  Pallas kernels  34.2 us (95%)
  local copies, waits for them, and re-layouts  1.57 us (4%)
    pallas_call x1, Pallas kernels, local(): pl.pallas_call(kernel, out_shape=jax.ShapeDtypeStruct((ROWS, CH), BF16),...  34.2 us
    unnamed x1, local copies, waits for them, and re-layouts  1.57 us

profile of v3, /device:TPU:1, one launch (start us, length us, event | category | flops | bytes accessed | tf_op | source)
XLA Modules:
  0.0 35.8 jit_solution(12158120721580516018)
XLA Ops:
  0.0 34.2 %hyena.1 = bf16[128,512]{1,0:T(8,128)(2,1)} custom-call(bf16[128,512]{1,0:T(8,128)(2,1)} %tokens.1, bf16[3,4096,512]{2,1,0:T(8,128)(2,1)} %bitcast.3, f32[3,7,512]{2,1,0:T(8,128)} %bitcast.4, bf16[2048,512]{1,0:T(8,128)(2,1)} %filters.1, f32[1,512]{1,0:T(1,128)} %bitcast.5, bf16[128,256]{1,0:T(8,128)(2,1)} %constant.8.clone.fwd_hi, ...), custom_call_target="tpu_custom_call" | custom-call | tf_op jit(solution)/shard_map/hyena/pallas_call | solution.py:482
  34.2 1.6 %copy.11 = bf16[128,512]{1,0:T(8,128)(2,1)} copy(bf16[128,512]{1,0:T(8,128)(2,1)} %hyena.1) | data formatting | bytes 262144

commit v4 on v3

--- a/solution.py
+++ b/solution.py
@@ -438,6 +438,10 @@
             halo_copy(src, dst, {"ctx": ctx, "tp": side}).wait_send()
 
 
+def hand_over(mixed, out):
+    out[...] = mixed[...]
+
+
 def local(tokens, in_weight, conv_weight, filters, skip_gain):
     any_space = pl.BlockSpec(memory_space=pl.ANY)
     dma = pltpu.SemaphoreType.DMA
@@ -479,7 +483,7 @@
         dma((NCTX,)),
         pltpu.SemaphoreType.REGULAR((3,)),
     ]
-    return pl.pallas_call(
+    mixed = pl.pallas_call(
         kernel,
         out_shape=jax.ShapeDtypeStruct((ROWS, CH), BF16),
         in_specs=[any_space] * 9,
@@ -497,6 +501,13 @@
         skip_gain.reshape(1, CH),
         *(jnp.asarray(table) for table in tables()),
     )
+    return pl.pallas_call(
+        hand_over,
+        out_shape=jax.ShapeDtypeStruct((ROWS, CH), BF16),
+        in_specs=[pl.BlockSpec(memory_space=pltpu.VMEM)],
+        out_specs=pl.BlockSpec(memory_space=pltpu.VMEM),
+        name="hand_over",
+    )(mixed)
 
 
 def solution(mesh):

time: 35.9 us -> 35.9 us (level)
  Pallas kernels: 34.2 us -> 35.8 us
  local copies, waits for them, and re-layouts: 1.57 us -> 0 us
    pallas_call x0 -> x1, Pallas kernels: none -> 1.57 us  [local(): pl.pallas_call(hand_over, out_shape=jax.ShapeDtypeStruct((ROWS, CH), BF16...]
    unnamed x1 -> x0, local copies, waits for them, and re-layouts: 1.57 us -> none
where the time goes in v4:
time: 35.9 us; the launch traced here: 35.8 us
  Pallas kernels  35.8 us (100%)
    pallas_call x1, Pallas kernels, local(): pl.pallas_call(kernel, out_shape=jax.ShapeDtypeStruct((ROWS, CH), BF16),...  34.2 us
    pallas_call x1, Pallas kernels, local(): pl.pallas_call(hand_over, out_shape=jax.ShapeDtypeStruct((ROWS, CH), BF16...  1.57 us

profile of v4, /device:TPU:1, one launch (start us, length us, event | category | flops | bytes accessed | tf_op | source)
XLA Modules:
  0.0 35.8 jit_solution(1793484050626503975)
XLA Ops:
  0.0 34.2 %hyena.1.mixed = bf16[128,512]{1,0:T(8,128)(2,1)} custom-call(bf16[128,512]{1,0:T(8,128)(2,1)} %tokens.1, bf16[3,4096,512]{2,1,0:T(8,128)(2,1)} %bitcast.3, f32[3,7,512]{2,1,0:T(8,128)} %bitcast.4, bf16[2048,512]{1,0:T(8,128)(2,1)} %filters.1, f32[1,512]{1,0:T(1,128)} %bitcast.5, bf16[128,256]{1,0:T(8,128)(2,1)} %constant.8.clone.fwd_hi, ...), custom_call_target="tpu_custom_call" | custom-call | tf_op jit(solution)/shard_map/hyena/pallas_call | solution.py:486
  34.2 1.6 %hand_over.1 = bf16[128,512]{1,0:T(8,128)(2,1)} custom-call(bf16[128,512]{1,0:T(8,128)(2,1)} %hyena.1.mixed), custom_call_target="tpu_custom_call" | custom-call | tf_op jit(solution)/shard_map/hand_over/pallas_call | solution.py:504

commit v5 on v3

--- a/solution.py
+++ b/solution.py
@@ -481,7 +481,7 @@
     ]
     return pl.pallas_call(
         kernel,
-        out_shape=jax.ShapeDtypeStruct((ROWS, CH), BF16),
+        out_shape=pltpu.VMEM((ROWS, CH), BF16),
         in_specs=[any_space] * 9,
         out_specs=pl.BlockSpec(memory_space=pltpu.VMEM),
         scratch_shapes=scratch,

time: 35.9 us -> 34.4 us (0.958)
  local copies, waits for them, and re-layouts: 1.57 us -> 0.66 us
  Pallas kernels: 34.2 us -> 33.7 us
    unnamed x1, local copies, waits for them, and re-layouts: 1.57 us -> 0.66 us
    pallas_call x1, Pallas kernels: 34.2 us -> 33.7 us  [local(): pl.pallas_call(kernel, out_shape=pltpu.VMEM((ROWS, CH), BF16), in_specs=[...]
where the time goes in v5:
time: 34.4 us; the launch traced here: 34.3 us
  Pallas kernels  33.7 us (98%)
  local copies, waits for them, and re-layouts  0.66 us (2%)
    pallas_call x1, Pallas kernels, local(): pl.pallas_call(kernel, out_shape=pltpu.VMEM((ROWS, CH), BF16), in_specs=[...  33.7 us

profile of v5, /device:TPU:1, one launch (start us, length us, event | category | flops | bytes accessed | tf_op | source)
XLA Modules:
  0.0 34.3 jit_solution(3477505626784161683)
XLA Ops:
  0.0 33.7 %hyena.1 = bf16[128,512]{1,0:T(8,128)(2,1)S(1)} custom-call(bf16[128,512]{1,0:T(8,128)(2,1)} %tokens.1, bf16[3,4096,512]{2,1,0:T(8,128)(2,1)} %bitcast.3, f32[3,7,512]{2,1,0:T(8,128)} %bitcast.4, bf16[2048,512]{1,0:T(8,128)(2,1)} %filters.1, f32[1,512]{1,0:T(1,128)} %bitcast.5, bf16[128,256]{1,0:T(8,128)(2,1)} %constant.8.clone.fwd_hi, ...), custom_call_target="tpu_custom_call" | custom-call | tf_op jit(solution)/shard_map/hyena/pallas_call | solution.py:482
  33.7 0.7 %copy.11 = bf16[128,512]{1,0:T(8,128)(2,1)} copy(bf16[128,512]{1,0:T(8,128)(2,1)S(1)} %hyena.1) | data formatting | bytes 262144
